TPU v7x, 32 devices: a whole 2x2x4 slice. The times are simulated.
32 devices in a mesh: dp: 4 (over y, core), seq: 8 (over z, x).
Axes of the slice: x: 2, y: 2, z: 4, core: 2. Of those that a mesh axis runs over, the one named last changes fastest.
Arguments:
- query: bfloat16 [8, 2048, 32, 128], P('dp', 'seq'), may hold values from -128 to 128
- keys: bfloat16 [8, 2048, 4, 128], P('dp', 'seq'), may hold values from -4.5 to 4.5
- values: bfloat16 [8, 2048, 4, 128], P('dp', 'seq'), may hold values from -6 to 6
- output: bfloat16 [8, 2048, 32, 128], P('dp', 'seq'), may hold values from -6 to 6
- out_grad: bfloat16 [8, 2048, 32, 128], P('dp', 'seq'), may hold values from -6 to 6
- lengths: int32 [8], P('dp'), may hold values from 341 to 2048, as said below
- margins: float32 [4], P('dp'), may hold values from -3 to 3
Outputs:
- query_grad: bfloat16 [8, 2048, 32, 128], P('dp', 'seq')
- key_grad: bfloat16 [8, 2048, 4, 128], P('dp', 'seq')
- value_grad: bfloat16 [8, 2048, 4, 128], P('dp', 'seq')
Inputs may be any that keep to these rules, and one draw needn't show every extreme that they name: `lengths`: sequence 2p is pair p's chosen response and 2p + 1 its rejected one; some sequence has exactly 2048 tokens.
All inputs are finite; a program needn't handle non-finite values.
Results may differ from a plain program's by a relative error of at most 0.009.
Values may be sent and summed in bfloat16 or wider, within the bound.
A program may use at most 128 MiB of HBM per device.

v0:
```python
import math

import jax
import jax.numpy as jnp
from jax import lax
from jax.sharding import PartitionSpec as P


def sequence_grads(query, scaled, keys, values, delta, length):
    full_len, per_dev, head_dim = query.shape
    slots = keys.shape[1]
    repeat = per_dev // slots
    block = min(512, full_len)
    scale = 1.0 / math.sqrt(head_dim)
    q_four = query.reshape(full_len, slots, repeat, head_dim)
    g_four = scaled.reshape(full_len, slots, repeat, head_dim)
    d_three = delta.reshape(full_len, slots, repeat)

    def make_step(start):
        prefix = start + block

        def one_block(carry):
            query_all, key_acc, value_acc = carry
            q_block = q_four[start:prefix]
            g_block = g_four[start:prefix]
            d_block = jnp.transpose(d_three[start:prefix], (1, 2, 0))[..., None]
            key_pre = keys[:prefix]
            value_pre = values[:prefix]
            scores = (
                jnp.einsum("isrd,jsd->srij", q_block, key_pre, preferred_element_type=jnp.float32)
                * scale
            )
            query_pos = start + jnp.arange(block)
            causal = jnp.arange(prefix)[None, :] <= query_pos[:, None]
            scores = jnp.where(causal, scores, -jnp.inf)
            top = jnp.max(scores, axis=-1, keepdims=True)
            lse = top + jnp.log(jnp.sum(jnp.exp(scores - top), axis=-1, keepdims=True))
            prob = jnp.exp(scores - lse)
            prob_low = prob.astype(jnp.bfloat16)
            value_part = jnp.einsum(
                "srij,isrd->jsd", prob_low, g_block, preferred_element_type=jnp.float32
            )
            dprob = jnp.einsum(
                "isrd,jsd->srij", g_block, value_pre, preferred_element_type=jnp.float32
            )
            dscore = prob * (dprob - d_block)
            dscore_low = dscore.astype(jnp.bfloat16)
            query_part = (
                jnp.einsum(
                    "srij,jsd->isrd", dscore_low, key_pre, preferred_element_type=jnp.float32
                )
                * scale
            )
            query_part = query_part.reshape(block, per_dev, head_dim).astype(jnp.bfloat16)
            query_all = lax.dynamic_update_slice_in_dim(query_all, query_part, start, 0)
            key_part = jnp.einsum(
                "srij,isrd->jsd", dscore_low, q_block, preferred_element_type=jnp.float32
            )
            key_acc = key_acc.at[:prefix].add(key_part)
            value_acc = value_acc.at[:prefix].add(value_part)
            return (query_all, key_acc, value_acc)

        return one_block

    carry = (
        jnp.zeros((full_len, per_dev, head_dim), jnp.bfloat16),
        jnp.zeros((full_len, slots, head_dim), jnp.float32),
        jnp.zeros((full_len, slots, head_dim), jnp.float32),
    )
    for index in range(full_len // block):
        start = index * block
        step_fn = make_step(start)
        carry = step_fn(carry)
    query_all, key_acc, value_acc = carry
    return (query_all, key_acc * scale, value_acc)


def body(query, keys, values, output, out_grad, lengths, margins):
    seq_size = lax.axis_size("seq")
    place = lax.axis_index("seq")
    seqs_dev, toks_dev, heads, head_dim = query.shape
    kv_heads = keys.shape[2]
    per_dev = heads // seq_size
    group = heads // kv_heads
    total = lax.psum(jnp.sum(lengths), "dp")
    mean_len = total.astype(jnp.float32) / (seqs_dev * lax.axis_size("dp"))
    weight = jax.nn.sigmoid(-margins)
    signs = jnp.tile(jnp.array([-1.0, 1.0], jnp.float32), margins.shape[0])
    coef = jnp.repeat(weight, 2) * signs * 4.0 * mean_len / lengths.astype(jnp.float32)
    positions = place * toks_dev + jnp.arange(toks_dev)
    live = (positions[None, :] < lengths[:, None]).astype(jnp.float32)
    factor = coef[:, None] * live
    scaled = (out_grad.astype(jnp.float32) * factor[:, :, None, None]).astype(jnp.bfloat16)
    copies = max(1, group // per_dev)
    key_slots = jnp.repeat(keys, copies, axis=2)
    value_slots = jnp.repeat(values, copies, axis=2)
    q_heads, g_heads, o_heads, k_heads, v_heads = (
        lax.all_to_all(query, "seq", split_axis=2, concat_axis=1, tiled=True),
        lax.all_to_all(scaled, "seq", split_axis=2, concat_axis=1, tiled=True),
        lax.all_to_all(output, "seq", split_axis=2, concat_axis=1, tiled=True),
        lax.all_to_all(key_slots, "seq", split_axis=2, concat_axis=1, tiled=True),
        lax.all_to_all(value_slots, "seq", split_axis=2, concat_axis=1, tiled=True),
    )
    delta = jnp.sum(g_heads.astype(jnp.float32) * o_heads.astype(jnp.float32), axis=3)
    query_heads, key_heads, value_heads = lax.map(
        lambda items: sequence_grads(*items), (q_heads, g_heads, k_heads, v_heads, delta, lengths)
    )
    query_grad = lax.all_to_all(query_heads, "seq", split_axis=1, concat_axis=2, tiled=True)
    key_rows, value_rows = (
        lax.all_to_all(key_heads, "seq", split_axis=1, concat_axis=2, tiled=True),
        lax.all_to_all(value_heads, "seq", split_axis=1, concat_axis=2, tiled=True),
    )
    key_grad = jnp.sum(
        key_rows.reshape(seqs_dev, toks_dev, kv_heads, copies, head_dim), axis=3
    ).astype(jnp.bfloat16)
    value_grad = jnp.sum(
        value_rows.reshape(seqs_dev, toks_dev, kv_heads, copies, head_dim), axis=3
    ).astype(jnp.bfloat16)
    return (query_grad, key_grad, value_grad)


def solution(mesh):
    return jax.shard_map(
        body,
        mesh=mesh,
        in_specs=(
            P("dp", "seq", None, None),
            P("dp", "seq", None, None),
            P("dp", "seq", None, None),
            P("dp", "seq", None, None),
            P("dp", "seq", None, None),
            P("dp"),
            P("dp"),
        ),
        out_specs=(
            P("dp", "seq", None, None),
            P("dp", "seq", None, None),
            P("dp", "seq", None, None),
        ),
        check_vma=False,
    )
```

profile of v0, /device:TPU:0, one launch (start us, length us, event | category | flops | bytes accessed | tf_op | source)
XLA Modules:
  0.0 792.0 jit_solution(2441812579054759764)
XLA Ops:
  3.0 7.3 all-to-all-start
  10.4 25.7 %all-to-all-done = bf16[2,256,8,128]{3,1,0,2:T(8,128)(2,1)S(1)} async-done(((bf16[2,256,8,128]{3,1,0,2:T(8,128)(2,1)}), bf16[2,256,8,128]{3,1,0,2:T(8,128)(2,1)S(1)}, u32[]{:S(2)}, u32[]{:S(2)}) %all-to-all-start) | async-done | bytes 1048608 | tf_op jit(solution)/shard_map/all_to_all | solution.py:101
  41.5 5.6 psum.7
  48.5 5.9 multiply_convert_fusion
  54.4 12.4 %all-to-all-done.2 = bf16[2,256,8,128]{3,1,0,2:T(8,128)(2,1)S(1)} async-done(((bf16[2,256,8,128]{3,1,0,2:T(8,128)(2,1)}), bf16[2,256,8,128]{3,1,0,2:T(8,128)(2,1)S(1)}, u32[]{:S(2)}, u32[]{:S(2)}) %all-to-all-start.2) | async-done | bytes 1048608 | tf_op jit(solution)/shard_map/all_to_all | solution.py:102
  71.3 5.8 copy.192
  77.2 86.7 %all-to-all-done.3 = bf16[2,256,32,128]{3,1,0,2:T(8,128)(2,1)} async-done(((bf16[2,256,32,128]{3,1,0,2:T(8,128)(2,1)}), bf16[2,256,32,128]{3,1,0,2:T(8,128)(2,1)}, u32[]{:S(2)}, u32[]{:S(2)}) %all-to-all-start.3) | async-done | bytes 4194336 | tf_op jit(solution)/shard_map/all_to_all | solution.py:99
  168.5 5.8 copy.198
  174.3 86.7 %all-to-all-done.1 = bf16[2,256,32,128]{3,1,0,2:T(8,128)(2,1)} async-done(((bf16[2,256,32,128]{3,1,0,2:T(8,128)(2,1)}), bf16[2,256,32,128]{3,1,0,2:T(8,128)(2,1)}, u32[]{:S(2)}, u32[]{:S(2)}) %all-to-all-start.1) | async-done | bytes 4194336 | tf_op jit(solution)/shard_map/all_to_all | solution.py:98
  277.2 80.9 %all-to-all-done.4 = bf16[2,256,32,128]{3,1,0,2:T(8,128)(2,1)} async-done(((bf16[2,256,32,128]{3,1,0,2:T(8,128)(2,1)}), bf16[2,256,32,128]{3,1,0,2:T(8,128)(2,1)}, u32[]{:S(2)}, u32[]{:S(2)}) %all-to-all-start.4) | async-done | bytes 4194336 | tf_op jit(solution)/shard_map/all_to_all | solution.py:100
  358.1 5.7 fusion.155
  363.9 221.8 %while.27 = (s32[]{:T(128)}, bf16[2,2048,4,128]{3,2,0,1:T(4,128)(2,1)}, f32[2,2048,1,128]{3,2,0,1:T(1,128)}, f32[2,2048,1,128]{3,2,0,1:T(1,128)}, bf16[2,2048,1,...) while((s32[]{:T(128)}, ...), condition=%wide.region_12.13_spmd, body=%wide.region_3.12_spmd.sunk | while | flops 13606184960 | bytes 444718720 | solution.py:105
  399.4 6.2 fusion.222
  405.6 5.7 fusion.215
  429.1 11.9 %fusion.223 = f32[1,2048,1,128]{1,3,2,0:T(8,128)} fusion(f32[2048,1,128]{0,2,1:T(8,128)} %fusion.222, f32[2048,512,4]{1,0,2:T(8,128)} %copy-done, f32[4,512]{1,0:T(4,128)S(1)} %log_add_fusion.11, pred[512,2048]{0,1:T(8,128)(4,1)S(1)} %copy-done.3, bf16[2,2048,4,128]{3,1,2,0:T(8,128)(2,1)} %get-tuple-element.461, s32[]{:T(128)S(6)} %copy.272, ...), kind=kOutput, calls=%fused_computation.58.clone.1 | convolution fusion | flops 1090781184 | bytes 20455432 | tf_op jit(solution)/shard_map/while/body/eval_jaxpr/srij,isrd->jsd/dot_general | solution.py:40
  441.0 9.0 %fusion.218 = bf16[4,512,2048]{1,2,0:T(8,128)(2,1)S(1)} fusion(f32[2048,512,4]{1,0,2:T(8,128)} %copy-done, f32[4,512]{1,0:T(4,128)S(1)} %get-tuple-element.420, f32[4,512]{1,0:T(4,128)S(1)} %log_add_fusion.11, pred[512,2048]{0,1:T(8,128)(4,1)S(1)} %copy-done.3, bf16[2,2048,1,128]{3,1,2,0:T(8,128)(2,1)S(1)} %copy-done.15, s32[]{:T(128)S(6)} %copy.272, ...), kind=kOutput, calls=%fused_computation.16.clone.1 | convolution fusion | flops 1098907648 | bytes 27280896 | tf_op jit(solution)/shard_map/while/body/eval_jaxpr/isrd,jsd->srij/dot_general | solution.py:43
  507.6 6.0 fusion.222
  513.6 5.7 fusion.215
  537.2 11.9 %fusion.223 = f32[1,2048,1,128]{1,3,2,0:T(8,128)} fusion(f32[2048,1,128]{0,2,1:T(8,128)} %fusion.222, f32[2048,512,4]{1,0,2:T(8,128)} %copy-done, f32[4,512]{1,0:T(4,128)S(1)} %log_add_fusion.11, pred[512,2048]{0,1:T(8,128)(4,1)S(1)} %copy-done.3, bf16[2,2048,4,128]{3,1,2,0:T(8,128)(2,1)} %get-tuple-element.461, s32[]{:T(128)S(6)} %copy.272, ...), kind=kOutput, calls=%fused_computation.58.clone.1 | convolution fusion | flops 1090781184 | bytes 20455432 | tf_op jit(solution)/shard_map/while/body/eval_jaxpr/srij,isrd->jsd/dot_general | solution.py:40
  549.1 9.0 %fusion.218 = bf16[4,512,2048]{1,2,0:T(8,128)(2,1)S(1)} fusion(f32[2048,512,4]{1,0,2:T(8,128)} %copy-done, f32[4,512]{1,0:T(4,128)S(1)} %get-tuple-element.420, f32[4,512]{1,0:T(4,128)S(1)} %log_add_fusion.11, pred[512,2048]{0,1:T(8,128)(4,1)S(1)} %copy-done.3, bf16[2,2048,1,128]{3,1,2,0:T(8,128)(2,1)S(1)} %copy-done.15, s32[]{:T(128)S(6)} %copy.272, ...), kind=kOutput, calls=%fused_computation.16.clone.1 | convolution fusion | flops 1098907648 | bytes 27280896 | tf_op jit(solution)/shard_map/while/body/eval_jaxpr/isrd,jsd->srij/dot_general | solution.py:43
  585.8 52.4 %all_to_all.129 = f32[2,2048,1,128]{3,2,0,1:T(1,128)} all-to-all(f32[2,2048,1,128]{3,2,0,1:T(1,128)} %get-tuple-element.269), channel_id=1, replica_groups=mesh['dp'=4,'seq'=8] {'seq'}, dimensions={1} | all-to-all | bytes 4194304 | tf_op jit(solution)/shard_map/all_to_all | solution.py:111
  638.2 51.2 %all_to_all.130 = f32[2,2048,1,128]{3,2,0,1:T(1,128)S(1)} all-to-all(f32[2,2048,1,128]{3,2,0,1:T(1,128)S(1)} %copy-done.14), channel_id=1, replica_groups=mesh['dp'=4,'seq'=8] {'seq'}, dimensions={1} | all-to-all | bytes 4194304 | tf_op jit(solution)/shard_map/all_to_all | solution.py:110
  702.8 83.4 %all-to-all-done.5 = bf16[2,2048,4,128]{3,2,0,1:T(4,128)(2,1)} async-done(((bf16[2,2048,4,128]{3,2,0,1:T(4,128)(2,1)}), bf16[2,2048,4,128]{3,2,0,1:T(4,128)(2,1)}, u32[]{:S(2)}, u32[]{:S(2)}) %all-to-all-start.5) | async-done | bytes 4194336 | tf_op jit(solution)/shard_map/all_to_all | solution.py:108
  786.2 5.6 copy.203
  (174 shorter events, 196.4 us)
Async XLA Ops:
  0.6 9.7 %copy-start.16 = (bf16[2,256,4,128]{3,2,1,0:T(4,128)(2,1)S(1)}, bf16[2,256,4,128]{3,2,1,0:T(4,128)(2,1)}, u32[]{:S(2)}) copy-start(bf16[2,256,4,128]{3,2,1,0:T(4,128)(2,1)} %param.32) | copy-start | bytes 1572868
  1.8 39.0 %copy-start.17 = (s32[2]{0:T(128)S(1)}, s32[2]{0:T(128)}, u32[]{:S(2)}) copy-start(s32[2]{0:T(128)} %param.35) | copy-start | bytes 28
  1.8 46.6 %copy-start.18 = (f32[2]{0:T(128)S(1)}, f32[2]{0:T(128)}, u32[]{:S(2)}) copy-start(f32[2]{0:T(128)} %constant.334.clone) | copy-start | bytes 28
  3.0 33.0 %all-to-all-start = ((bf16[2,256,8,128]{3,1,0,2:T(8,128)(2,1)}), bf16[2,256,8,128]{3,1,0,2:T(8,128)(2,1)S(1)}, u32[]{:S(2)}, u32[]{:S(2)}) async-start(bf16[2,256,8,128]{3,1,0,2:T(8,128)(2,1)} %bitcast.103), calls=%async_computation | async-start | bytes 2097152 | tf_op jit(solution)/shard_map/all_to_all | solution.py:101
  37.2 29.5 %all-to-all-start.2 = ((bf16[2,256,8,128]{3,1,0,2:T(8,128)(2,1)}), bf16[2,256,8,128]{3,1,0,2:T(8,128)(2,1)S(1)}, u32[]{:S(2)}, u32[]{:S(2)}) async-start(bf16[2,256,8,128]{3,1,0,2:T(8,128)(2,1)} %bitcast.628), calls=%async_computation.2 | async-start | bytes 2097152 | tf_op jit(solution)/shard_map/all_to_all | solution.py:102
  66.8 10.4 %copy-start.11 = (bf16[2,256,8,128]{3,1,0,2:T(8,128)(2,1)}, bf16[2,256,8,128]{3,1,0,2:T(8,128)(2,1)S(1)}, u32[]{:S(2)}) copy-start(bf16[2,256,8,128]{3,1,0,2:T(8,128)(2,1)S(1)} %all-to-all-done.2) | copy-start | bytes 3145732
  66.8 97.1 %all-to-all-start.3 = ((bf16[2,256,32,128]{3,1,0,2:T(8,128)(2,1)}), bf16[2,256,32,128]{3,1,0,2:T(8,128)(2,1)}, u32[]{:S(2)}, u32[]{:S(2)}) async-start(bf16[2,256,32,128]{3,1,0,2:T(8,128)(2,1)} %multiply_convert_fusion), calls=%async_computation.3 | async-start | bytes 8388608 | tf_op jit(solution)/shard_map/all_to_all | solution.py:99
  163.9 97.1 %all-to-all-start.1 = ((bf16[2,256,32,128]{3,1,0,2:T(8,128)(2,1)}), bf16[2,256,32,128]{3,1,0,2:T(8,128)(2,1)}, u32[]{:S(2)}, u32[]{:S(2)}) async-start(bf16[2,256,32,128]{3,1,0,2:T(8,128)(2,1)} %copy.192), calls=%async_computation.1 | async-start | bytes 8388608 | tf_op jit(solution)/shard_map/all_to_all | solution.py:98
  261.0 97.1 %all-to-all-start.4 = ((bf16[2,256,32,128]{3,1,0,2:T(8,128)(2,1)}), bf16[2,256,32,128]{3,1,0,2:T(8,128)(2,1)}, u32[]{:S(2)}, u32[]{:S(2)}) async-start(bf16[2,256,32,128]{3,1,0,2:T(8,128)(2,1)} %copy.198), calls=%async_computation.4 | async-start | bytes 8388608 | tf_op jit(solution)/shard_map/all_to_all | solution.py:100
  364.3 30.1 %copy-start.6 = (bf16[2,2048,1,128]{3,1,2,0:T(8,128)(2,1)}, bf16[2,2048,1,128]{3,1,2,0:T(8,128)(2,1)S(1)}, u32[]{:S(2)}) copy-start(bf16[2,2048,1,128]{3,1,2,0:T(8,128)(2,1)S(1)} %get-tuple-element.458) | copy-start | bytes 3145732 | tf_op jit(solution)/shard_map/while
  365.4 34.0 %copy-start.9 = (pred[512,1536]{0,1:T(8,128)(4,1)}, pred[512,1536]{0,1:T(8,128)(4,1)S(1)}, u32[]{:S(2)}) copy-start(pred[512,1536]{0,1:T(8,128)(4,1)S(1)} %iota_compare_fusion.10) | copy-start | bytes 2359300 | tf_op jit(solution)/shard_map/while
  423.4 5.7 copy-start
  429.1 11.9 %copy-start.15 = (bf16[2,2048,1,128]{3,1,2,0:T(8,128)(2,1)S(1)}, bf16[2,2048,1,128]{3,1,2,0:T(8,128)(2,1)}, u32[]{:S(2)}) copy-start(bf16[2,2048,1,128]{3,1,2,0:T(8,128)(2,1)} %get-tuple-element.460) | copy-start | bytes 3145732 | tf_op jit(solution)/shard_map/while
  441.0 9.0 %copy-start.2 = (f32[2048,1,128]{0,2,1:T(8,128)S(1)}, f32[2048,1,128]{0,2,1:T(8,128)}, u32[]{:S(2)}) copy-start(f32[2048,1,128]{0,2,1:T(8,128)} %fusion.226) | copy-start | bytes 3145732 | tf_op jit(solution)/shard_map/while
  450.1 5.0 copy-start.7
  472.3 30.3 %copy-start.6 = (bf16[2,2048,1,128]{3,1,2,0:T(8,128)(2,1)}, bf16[2,2048,1,128]{3,1,2,0:T(8,128)(2,1)S(1)}, u32[]{:S(2)}) copy-start(bf16[2,2048,1,128]{3,1,2,0:T(8,128)(2,1)S(1)} %get-tuple-element.458) | copy-start | bytes 3145732 | tf_op jit(solution)/shard_map/while
  473.4 34.2 %copy-start.9 = (pred[512,1536]{0,1:T(8,128)(4,1)}, pred[512,1536]{0,1:T(8,128)(4,1)S(1)}, u32[]{:S(2)}) copy-start(pred[512,1536]{0,1:T(8,128)(4,1)S(1)} %iota_compare_fusion.10) | copy-start | bytes 2359300 | tf_op jit(solution)/shard_map/while
  531.4 5.7 copy-start
  537.1 11.9 %copy-start.15 = (bf16[2,2048,1,128]{3,1,2,0:T(8,128)(2,1)S(1)}, bf16[2,2048,1,128]{3,1,2,0:T(8,128)(2,1)}, u32[]{:S(2)}) copy-start(bf16[2,2048,1,128]{3,1,2,0:T(8,128)(2,1)} %get-tuple-element.460) | copy-start | bytes 3145732 | tf_op jit(solution)/shard_map/while
  549.1 9.0 %copy-start.2 = (f32[2048,1,128]{0,2,1:T(8,128)S(1)}, f32[2048,1,128]{0,2,1:T(8,128)}, u32[]{:S(2)}) copy-start(f32[2048,1,128]{0,2,1:T(8,128)} %fusion.226) | copy-start | bytes 3145732 | tf_op jit(solution)/shard_map/while
  558.1 5.0 copy-start.7
  577.0 3.1 copy-start.8
  585.8 52.4 %copy-start.14 = (f32[2,2048,1,128]{3,2,0,1:T(1,128)S(1)}, f32[2,2048,1,128]{3,2,0,1:T(1,128)}, u32[]{:S(2)}) copy-start(f32[2,2048,1,128]{3,2,0,1:T(1,128)} %get-tuple-element.268) | copy-start | bytes 6291460
  689.4 96.8 %all-to-all-start.5 = ((bf16[2,2048,4,128]{3,2,0,1:T(4,128)(2,1)}), bf16[2,2048,4,128]{3,2,0,1:T(4,128)(2,1)}, u32[]{:S(2)}, u32[]{:S(2)}) async-start(bf16[2,2048,4,128]{3,2,0,1:T(4,128)(2,1)} %get-tuple-element.267), calls=%async_computation.5 | async-start | bytes 8388608 | tf_op jit(solution)/shard_map/all_to_all | solution.py:108
  (15 other events, 33.5 us)
where the time goes:
time: 801 us; the launch traced here: 792 us
  waiting for transfers between devices  376 us (47%)
  matrix products  149 us (19%)
  blocking collectives  109 us (14%)
  local copies, waits for them, and re-layouts  77.2 us (10%)
  other arithmetic  42.7 us (5%)
  starting transfers between devices  29.1 us (4%)
    all_to_all x1, waiting for transfers between devices, body(): lax.all_to_all(query, 'seq', split_axis=2, concat_axis=1, tiled=True)  86.7 us
    all_to_all x1, waiting for transfers between devices, body(): lax.all_to_all(scaled, 'seq', split_axis=2, concat_axis=1, tiled=True)  86.7 us
    all_to_all x1, waiting for transfers between devices, body(): lax.all_to_all(query_heads, 'seq', split_axis=1, concat_axis=2, tiled=True)  83.4 us
    all_to_all x1, waiting for transfers between devices, body(): lax.all_to_all(output, 'seq', split_axis=2, concat_axis=1, tiled=True)  80.9 us
    all_to_all x1, blocking collectives, body(): lax.all_to_all(value_heads, 'seq', split_axis=1, concat_axis=2, tiled=True)  52.4 us
    all_to_all x1, blocking collectives, body(): lax.all_to_all(key_heads, 'seq', split_axis=1, concat_axis=2, tiled=True)  51.2 us
    dot_general x8, matrix products, one_block(): jnp.einsum('srij,isrd->jsd', prob_low, g_block, preferred_element_type=jn...  47.3 us
    dot_general x8, matrix products, one_block(): jnp.einsum('isrd,jsd->srij', g_block, value_pre, preferred_element_type=j...  42.4 us
  transfers between devices with their start and end apart: 6, of which 6 were waited for; matrix products, arithmetic and copies ran while one was open for 5% of the time, Pallas kernels for 0%

commit v1 on v0

v1 whole, which is shorter than its diff:
```python
import functools
import math

import jax
import jax.numpy as jnp
from jax import lax
from jax.experimental import pallas as pl
from jax.experimental.pallas import tpu as pltpu
from jax.sharding import PartitionSpec as P

CHUNK_TOKENS = 64
LOW = -1e30


def attend_kernel(
    info,
    coef,
    query_ref,
    grad_ref,
    output_ref,
    kv_ref,
    *rest,
    scale,
    seq,
    chunk_tokens,
):
    query_grad_ref, kv_grad_ref, e_ref, m_ref, key_acc, value_acc, wide_ref = rest[-7:]
    toks, group, dim = query_ref.shape[1:]
    places = kv_ref.shape[0]
    rows = chunk_tokens * group
    place = info[0]
    length = info[1 + seq]
    factor_live = coef[seq]
    base = place * toks
    log2e = scale * math.log2(math.e)

    lane = lax.broadcasted_iota(jnp.int32, (toks, dim), 1)
    ones = jnp.where(lane < 3, 1.0, 0.0).astype(jnp.bfloat16)

    def zero_rest(j, _):
        kv_grad_ref[j] = jnp.zeros(kv_grad_ref.shape[1:], kv_grad_ref.dtype)
        return 0

    def prepare(j, _):
        key_acc[j] = jnp.zeros((toks, dim), jnp.float32)
        value_acc[j] = jnp.zeros((toks, dim), jnp.float32)
        wide_ref[j, :, :dim] = kv_ref[j, 0, 0, 1]
        wide_ref[j, :, dim:] = ones
        return 0

    lax.fori_loop(0, place + 1, prepare, 0)

    def chunk(c, _):
        tok0 = pl.multiple_of(c * chunk_tokens, chunk_tokens)
        here = pl.ds(tok0, chunk_tokens)

        @pl.when(base + tok0 >= length)
        def _():
            query_grad_ref[0, here] = jnp.zeros((chunk_tokens, group, dim), query_grad_ref.dtype)

        @pl.when(base + tok0 < length)
        def _():
            q = (
                query_ref[0, here].astype(jnp.float32).reshape(rows, dim).astype(jnp.bfloat16)
            )
            position = (
                base + tok0 + lax.broadcasted_iota(jnp.int32, (chunk_tokens, group, dim), 0)
            )
            factor = jnp.where(position < length, factor_live, 0.0)
            g = (grad_ref[0, here].astype(jnp.float32) * factor).reshape(rows, dim)
            g_low = g.astype(jnp.bfloat16)
            o = output_ref[0, here].astype(jnp.float32).reshape(rows, dim)
            delta = jnp.sum(g_low.astype(jnp.float32) * o, axis=-1, keepdims=True)
            high = delta.astype(jnp.bfloat16).astype(jnp.float32)
            middle = (delta - high).astype(jnp.bfloat16).astype(jnp.float32)
            low = delta - high - middle
            row_lane = lax.broadcasted_iota(jnp.int32, (rows, dim), 1)
            extra = jnp.where(
                row_lane == 0,
                -high,
                jnp.where(row_lane == 1, -middle, jnp.where(row_lane == 2, -low, 0.0)),
            ).astype(jnp.bfloat16)
            g_wide = jnp.concatenate([g_low, extra], axis=1)

            def scores_of(j):
                return lax.dot_general(
                    kv_ref[j, 0, 0, 0],
                    q,
                    (((1,), (1,)), ((), ())),
                    preferred_element_type=jnp.float32,
                )

            def absorb(j, s, carry):
                top, total = carry
                new = jnp.maximum(top, jnp.max(s, axis=0, keepdims=True) * log2e)
                e = jnp.exp2(s * log2e - new)
                e_ref[j] = e
                m_ref[j] = new
                total = total * jnp.exp2(top - new) + jnp.sum(e, axis=0, keepdims=True)
                return (new, total)

            carry = (jnp.full((1, rows), LOW, jnp.float32), jnp.zeros((1, rows), jnp.float32))
            carry = lax.fori_loop(0, place, lambda j, x: absorb(j, scores_of(j), x), carry)
            key_pos = lax.broadcasted_iota(jnp.int32, (toks, rows), 0)
            row_pos = tok0 + lax.broadcasted_iota(jnp.int32, (toks, rows), 1) // group
            top, total = absorb(
                place, jnp.where(key_pos <= row_pos, scores_of(place), LOW), carry
            )
            inverse = 1.0 / total

            def back(j, acc):
                prob = e_ref[j] * (jnp.exp2(m_ref[j] - top) * inverse)
                value_acc[j] += jnp.dot(
                    prob.astype(jnp.bfloat16), g_low, preferred_element_type=jnp.float32
                )
                dprob = lax.dot_general(
                    wide_ref[j],
                    g_wide,
                    (((1,), (1,)), ((), ())),
                    preferred_element_type=jnp.float32,
                )
                dscore = (prob * dprob).astype(jnp.bfloat16)
                key_acc[j] += jnp.dot(dscore, q, preferred_element_type=jnp.float32)
                return acc + lax.dot_general(
                    dscore,
                    kv_ref[j, 0, 0, 0],
                    (((0,), (0,)), ((), ())),
                    preferred_element_type=jnp.float32,
                )

            acc = lax.fori_loop(0, place + 1, back, jnp.zeros((rows, dim), jnp.float32))
            query_grad_ref[0, here] = (
                (acc * scale).reshape(chunk_tokens, group, dim).astype(query_grad_ref.dtype)
            )

        return 0

    lax.fori_loop(0, toks // chunk_tokens, chunk, 0)

    def finish(j, _):
        kv_grad_ref[j, 0, 0] = (key_acc[j] * scale).astype(kv_grad_ref.dtype)
        kv_grad_ref[j, 0, 1] = value_acc[j].astype(kv_grad_ref.dtype)
        return 0

    lax.fori_loop(0, place + 1, finish, 0)
    lax.fori_loop(place + 1, places, zero_rest, 0)


def attend(info, coef, query, grad, output, kv, seq, first, carry):
    seqs, toks, heads, dim = query.shape
    places, _, count = kv.shape[:3]
    kv_all = carry[1]
    group = heads // kv_all
    chunk_tokens = min(CHUNK_TOKENS, toks)
    rows = chunk_tokens * group
    token_spec = pl.BlockSpec((1, toks, group, dim), lambda h, *_: (seq, 0, first + h, 0))
    kv_spec = pl.BlockSpec((places, 1, 1, 2, toks, dim), lambda h, *_: (0, 0, h, 0, 0, 0))
    grad_spec = pl.BlockSpec((places, 1, 2, toks, dim), lambda h, *_: (0, h, 0, 0, 0))
    operands = [info, coef, query, grad, output, kv]
    in_specs = [token_spec, token_spec, token_spec, kv_spec]
    aliases = {}
    if carry[0] is not None:
        aliases = {len(operands): 0}
        operands.append(carry[0])
        in_specs.append(pl.BlockSpec(memory_space=pl.ANY))
    flops = 5 * 2 * heads // kv_all * count * toks * toks * places * dim
    return pl.pallas_call(
        functools.partial(
            attend_kernel,
            scale=1.0 / math.sqrt(dim),
            seq=seq,
            chunk_tokens=chunk_tokens,
        ),
        out_shape=(
            jax.ShapeDtypeStruct(query.shape, query.dtype),
            jax.ShapeDtypeStruct((places, count, 2, toks, dim), jnp.bfloat16),
        ),
        grid_spec=pltpu.PrefetchScalarGridSpec(
            num_scalar_prefetch=2,
            grid=(count,),
            in_specs=in_specs,
            out_specs=(token_spec, grad_spec),
            scratch_shapes=[
                pltpu.VMEM((places, toks, rows), jnp.float32),
                pltpu.VMEM((places, 1, rows), jnp.float32),
                pltpu.VMEM((places, toks, dim), jnp.float32),
                pltpu.VMEM((places, toks, dim), jnp.float32),
                pltpu.VMEM((places, toks, 2 * dim), jnp.bfloat16),
            ],
        ),
        input_output_aliases=aliases,
        cost_estimate=pl.CostEstimate(
            flops=flops,
            bytes_accessed=4 * 2 * toks * group * count * dim * 2,
            transcendentals=0,
        ),
        compiler_params=pltpu.CompilerParams(vmem_limit_bytes=48 * 1024 * 1024),
    )(*operands)


def body(query, keys, values, output, out_grad, lengths, margins):
    place = lax.axis_index("seq")
    seqs, toks, heads, dim = query.shape
    kv_heads = keys.shape[2]
    kv = jnp.stack([keys, values], axis=1).transpose(0, 3, 1, 2, 4)
    split = 1
    step = kv_heads // split
    gathered = {
        (s, c): lax.all_gather(kv[s : s + 1, c : c + step], "seq", axis=0, tiled=False)
        for s in range(seqs)
        for c in range(0, kv_heads, step)
    }
    total = lax.psum(jnp.sum(lengths), "dp")
    mean_len = total.astype(jnp.float32) / (seqs * lax.axis_size("dp"))
    weight = jax.nn.sigmoid(-margins)
    signs = jnp.tile(jnp.array([-1.0, 1.0], jnp.float32), margins.shape[0])
    coef = jnp.repeat(weight, 2) * signs * 4.0 * mean_len / lengths.astype(jnp.float32)
    info = jnp.concatenate([place[None].astype(jnp.int32), lengths.astype(jnp.int32)])
    query_grad = None
    parts = []
    for s in range(seqs):
        row = []
        for c in range(0, kv_heads, step):
            query_grad, kv_grad = attend(
                info, coef, query, out_grad, output, gathered[s, c], s, c, (query_grad, kv_heads)
            )
            row.append(lax.psum_scatter(kv_grad, "seq", scatter_dimension=0, tiled=False))
        parts.append(jnp.concatenate(row, axis=0) if split > 1 else row[0])
    grads = jnp.stack(parts)
    key_grad = grads[:, :, 0].transpose(0, 2, 1, 3)
    value_grad = grads[:, :, 1].transpose(0, 2, 1, 3)
    return (query_grad, key_grad, value_grad)


def solution(mesh):
    tokens = P("dp", "seq", None, None)
    return jax.shard_map(
        body,
        mesh=mesh,
        in_specs=(tokens,) * 5 + (P("dp"), P("dp")),
        out_specs=(tokens,) * 3,
        check_vma=False,
    )
```

time: 801 us -> 410 us (0.51); the launches traced: 792 us -> 410 us
  matrix products: 149 us -> 0 us
  blocking collectives: 109 us -> 7.11 us
  local copies, waits for them, and re-layouts: 77.2 us -> 11 us
  waiting for transfers between devices: 376 us -> 328 us
  Pallas kernels: 0 us -> 47.2 us
  other arithmetic: 42.7 us -> 0.81 us
  starting transfers between devices: 29.1 us -> 0.16 us
  between operations: 2.36 us -> 15.2 us
    all_to_all x6 -> x0, waiting for transfers between devices: 376 us -> none  [the longest x1 86.7 us: body(): lax.all_to_all(query, 'seq', split_axis=2, concat_axis=1, tiled=True)]
    reduce_scatter x0 -> x2, waiting for transfers between devices: none -> 213 us  [body(): lax.psum_scatter(kv_grad, 'seq', scatter_dimension=0, tiled=False)]
    dot_general x40 -> x0, matrix products: 149 us -> none  [the longest x8 47.3 us: one_block(): jnp.einsum('srij,isrd->jsd', prob_low, g_block, preferred_element_type=jn...]
    all_gather x0 -> x2, waiting for transfers between devices: none -> 115 us  [body(): lax.all_gather(kv[s:s + 1, c:c + step], 'seq', axis=0, tiled=False)]
    all_to_all x2 -> x0, blocking collectives: 104 us -> none  [the longest x1 52.4 us: body(): lax.all_to_all(value_heads, 'seq', split_axis=1, concat_axis=2, tiled=True)]
    pallas_call x0 -> x2, Pallas kernels: none -> 47.2 us  [attend(): pl.pallas_call(functools.partial(attend_kernel, scale=1.0 / math.sqrt(dim...]
    reduce_sum x11 -> x0, other arithmetic: 30.3 us -> none  [the longest x8 19.2 us: one_block(): lse = top + jnp.log(jnp.sum(jnp.exp(scores - top), axis=-1, keepdims=True))]
    all_to_all x6 -> x0, starting transfers between devices: 29.1 us -> none  [the longest x1 7.28 us: body(): lax.all_to_all(key_slots, 'seq', split_axis=2, concat_axis=1, tiled=True)]
  transfers between devices with their start and end apart: 6 -> 4, of which waited for: 6 -> 4; matrix products, arithmetic and copies ran while one was open for 5% -> 0% of each run, Pallas kernels for 0% -> 12%
where the time goes in v1:
time: 410 us
  waiting for transfers between devices  328 us (80%)
  Pallas kernels  47.2 us (12%)
  between operations  15.2 us (4%)
  local copies, waits for them, and re-layouts  11 us (3%)
  blocking collectives  7.11 us (2%)
    reduce_scatter x2, waiting for transfers between devices, body(): lax.psum_scatter(kv_grad, 'seq', scatter_dimension=0, tiled=False)  213 us
    all_gather x2, waiting for transfers between devices, body(): lax.all_gather(kv[s:s + 1, c:c + step], 'seq', axis=0, tiled=False)  115 us
    pallas_call x2, Pallas kernels, attend(): pl.pallas_call(functools.partial(attend_kernel, scale=1.0 / math.sqrt(dim...  47.2 us
  transfers between devices with their start and end apart: 4, of which 4 were waited for; matrix products, arithmetic and copies ran while one was open for 0% of the time, Pallas kernels for 12%

profile of v1, /device:TPU:0, one launch (start us, length us, event | category | flops | bytes accessed | tf_op | source)
XLA Modules:
  0.0 409.6 jit_solution(9727832779804931560)
XLA Ops:
  7.2 0.0 all-gather.7.cloned.1.call-start
  7.2 1.4 copy_bitcast_fusion
  8.6 0.1 maximum_bitcast_fusion
  8.7 1.0 fusion
  9.8 0.0 all-gather.5.cloned.1.call-start
  9.9 0.7 all-gather.5.cloned.1.call-update
  10.6 0.0 reduce-scatter.3.cloned.1.call-start
  10.6 0.6 reduce_sum.9
  11.3 7.1 %psum.7 = s32[]{:T(128)} all-reduce(s32[]{:T(128)} %reduce_sum.9), channel_id=1, replica_groups=mesh['dp'=4,'seq'=8] {'dp'}, use_global_device_ids=true, to_apply=%region_1.0 | all-reduce | flops 1 | bytes 8 | tf_op jit(solution)/shard_map/psum | solution.py:213
  19.8 0.1 pad_add_fusion.info
  19.9 66.4 %all-gather.7.cloned.1.call-done = bf16[8,4,2,256,128]{4,3,2,1,0:T(8,128)(2,1)} async-done(((bf16[1,4,2,256,128]{4,3,2,1,0:T(8,128)(2,1)}), bf16[8,4,2,256,128]{4,3,2,1,0:T(8,128)(2,1)}) %all-gather.7.cloned.1.call-update) | async-done | bytes 4194320 | tf_op jit(solution)/shard_map/all_gather | solution.py:209
  86.2 23.6 %shard_map.103 = (bf16[2,256,32,128]{3,2,1,0:T(8,128)(2,1)}, bf16[8,4,2,256,128]{4,3,2,1,0:T(8,128)(2,1)S(1)}) custom-call(s32[3]{0:T(128)S(1)} %pad_add_fusion.info, f32[2]{0:T(128)S(1)} %convert_divide_fusion.coef, bf16[2,256,32,128]{3,2,1,0:T(8,128)(2,1)} %query_ref.3, bf16[2,256,32,128]{3,2,1,0:T(8,128)(2,1)} %grad_ref.3, ...), custom_call_target="tpu_custom_call" | custom-call | flops 21474836480 | bytes 16777216 | tf_op jit(solution)/shard_map/pallas_call | solution.py:167
  109.8 2.0 copy-done
  111.8 0.0 reduce-scatter.5.cloned.1.call-start
  111.9 48.4 %all-gather.5.cloned.1.call-done = bf16[8,4,2,256,128]{4,3,2,1,0:T(8,128)(2,1)} async-done(((bf16[1,4,2,256,128]{4,3,2,1,0:T(8,128)(2,1)}), bf16[8,4,2,256,128]{4,3,2,1,0:T(8,128)(2,1)}) %all-gather.5.cloned.1.call-update) | async-done | bytes 4194320 | tf_op jit(solution)/shard_map/all_gather | solution.py:209
  160.3 23.6 %shard_map.104 = (bf16[2,256,32,128]{3,2,1,0:T(8,128)(2,1)}, bf16[8,4,2,256,128]{4,3,2,1,0:T(8,128)(2,1)S(1)}) custom-call(s32[3]{0:T(128)S(1)} %pad_add_fusion.info, f32[2]{0:T(128)S(1)} %convert_divide_fusion.coef, bf16[2,256,32,128]{3,2,1,0:T(8,128)(2,1)} %query_ref.3, bf16[2,256,32,128]{3,2,1,0:T(8,128)(2,1)} %grad_ref.3, ...), custom_call_target="tpu_custom_call", output_to_operand_aliasing={{0}: (6, {})} | custom-call | flops 21474836480 | bytes 16777216 | tf_op jit(solution)/shard_map/pallas_call | solution.py:167
  183.9 1.9 copy-done.1
  185.9 122.2 %reduce-scatter.3.cloned.1.call-done = bf16[1,4,2,256,128]{4,3,2,1,0:T(8,128)(2,1)} async-done(((bf16[8,4,2,256,128]{4,3,2,1,0:T(8,128)(2,1)}), bf16[1,4,2,256,128]{4,3,2,1,0:T(8,128)(2,1)}) %reduce-scatter.3.cloned.1.call-update) | async-done | bytes 524304 | tf_op jit(solution)/shard_map/reduce_scatter | solution.py:227
  308.1 1.1 constant_dynamic-update-slice_fusion.1
  309.1 90.4 %reduce-scatter.5.cloned.1.call-done = bf16[1,4,2,256,128]{4,3,2,1,0:T(8,128)(2,1)} async-done(((bf16[8,4,2,256,128]{4,3,2,1,0:T(8,128)(2,1)}), bf16[1,4,2,256,128]{4,3,2,1,0:T(8,128)(2,1)}) %reduce-scatter.5.cloned.1.call-update) | async-done | bytes 524304 | tf_op jit(solution)/shard_map/reduce_scatter | solution.py:227
  399.5 1.1 constant_dynamic-update-slice_fusion
  400.6 0.1 slice_bitcast_fusion
  400.7 1.2 copy.20
  401.9 1.2 copy.19
  (10 shorter events, 0.1 us)
Async XLA Ops:
  7.2 12.7 %copy-start.3 = (f32[2]{0:T(128)S(1)}, f32[2]{0:T(128)}, u32[]{:S(2)}) copy-start(f32[2]{0:T(128)} %constant.15.clone) | copy-start | bytes 28
  7.2 3.4 copy-start.2
  7.2 79.0 %all-gather.7.cloned.1.call-start = ((), (), s32[]{:S(2)}) async-start(), calls=%async_computation.5 | async-start | bytes 4718592 | tf_op jit(solution)/shard_map/all_gather | solution.py:209
  9.8 150.5 %all-gather.5.cloned.1.call-start = ((), (), s32[]{:S(2)}) async-start(), calls=%async_computation.4 | async-start | bytes 4718592 | tf_op jit(solution)/shard_map/all_gather | solution.py:209
  10.6 297.5 %reduce-scatter.3.cloned.1.call-start = ((), (), s32[]{:S(2)}) async-start(), calls=%async_computation.2 | async-start | bytes 4718592 | tf_op jit(solution)/shard_map/reduce_scatter | solution.py:227
  109.8 2.0 copy-start
  111.8 287.7 %reduce-scatter.5.cloned.1.call-start = ((), (), s32[]{:S(2)}) async-start(), calls=%async_computation.3 | async-start | bytes 4718592 | tf_op jit(solution)/shard_map/reduce_scatter | solution.py:227
  183.9 1.9 copy-start.1
Sparse Core Ops, SparseCore 0:
  10.7 75.4 all-gather.6
  88.9 71.3 all-gather.4
  163.9 144.0 reduce-scatter.2
  311.5 87.9 reduce-scatter.4
